TPU v7x, 32 devices: a whole 2x2x4 slice. The times are simulated.
32 devices in a mesh: patch: 8 (over y, x, core), group: 4 (over z).
Axes of the slice: x: 2, y: 2, z: 4, core: 2. Of those that a mesh axis runs over, the one named last changes fastest.
Arguments:
- grid_latent: bfloat16 [16384, 512], P(('patch', 'group')), may hold values from -6 to 6
- mesh_latent: bfloat16 [8192, 512], P(('patch', 'group')), may hold values from -6 to 6
- cotangent: bfloat16 [8192, 512], P(('patch', 'group')), may hold values from -6 to 6
- halo_rows: int32 [8192], P(('patch', 'group')), may hold values from 0 to 511
- encoder_sender: int32 [24576], P(('patch', 'group')), may hold values from 0 to 767
- encoder_target: int32 [24576], P(('patch', 'group')), may hold values from 0 to 255
- encoder_count: int32 [32], P(('patch', 'group')), may hold values from 96 to 768, as said below
- process_sender: int32 [24576], P(('patch', 'group')), may hold values from 0 to 319
- process_target: int32 [24576], P(('patch', 'group')), may hold values from 0 to 255
- process_count: int32 [32], P(('patch', 'group')), may hold values from 96 to 768, as said below
- encoder_source: bfloat16 [512, 512], replicated, may hold values from -0.25 to 0.25
- encoder_dest: bfloat16 [512, 512], replicated, may hold values from -0.25 to 0.25
- encoder_output: bfloat16 [512, 512], replicated, may hold values from -0.25 to 0.25
- encoder_gain: float32 [512], replicated, may hold values from 0.5 to 1.5
- process_source: bfloat16 [512, 512], replicated, may hold values from -0.25 to 0.25
- process_dest: bfloat16 [512, 512], replicated, may hold values from -0.25 to 0.25
- process_output: bfloat16 [512, 512], replicated, may hold values from -0.25 to 0.25
- process_gain: float32 [512], replicated, may hold values from 0.5 to 1.5
Outputs:
- grid_grad: bfloat16 [16384, 512], P(('patch', 'group'))
- mesh_grad: bfloat16 [8192, 512], P(('patch', 'group'))
Inputs may be any that keep to these rules, and one draw needn't show every extreme that they name: `halo_rows`: a block's entries are rows of its own grid nodes. `encoder_sender`: rows of the block's extended grid table. `encoder_target`: rows of the block's own mesh nodes. The first encoder_count slots of a block are edges, the rest padding; some block is full in every draw. `process_sender`: rows of the block's sender table: its own mesh nodes, then the coarse nodes of its group. `process_target`: rows of the block's own mesh nodes. The first process_count slots of a block are edges, the rest padding; some block is full in every draw.
All inputs are finite; a program needn't handle non-finite values.
Results may differ from a plain program's by a relative error of at most 0.01.
Values may be sent and summed in bfloat16 or wider, within the bound.
No kernel may reach another device: no remote copies, remote signals or barrier semaphores. Data moves between devices by JAX's collectives and lax.ppermute only.
A program may use at most 64 MiB of HBM per device.

v0:
```python
import jax
import jax.numpy as jnp
from jax import lax
from jax.sharding import PartitionSpec as P

EPSILON = 1e-05


def padded_2(x, sides, width):
    for axis, dim in sides:
        size, length = (lax.axis_size(axis), x.shape[dim])
        up = [(i, (i + 1) % size) for i in range(size)]
        down = [(j, i) for i, j in up]
        last = lax.slice_in_dim(x, length - width, length, axis=dim)
        initial = lax.slice_in_dim(x, 0, width, axis=dim)
        before = lax.ppermute(last, axis, up)
        after = lax.ppermute(initial, axis, down)
        x = jnp.concatenate([before, x, after], axis=dim)
    return x


def silu_slope(values):
    logistic = jax.nn.sigmoid(values)
    return logistic * (1.0 + values * (1.0 - logistic))


def norm_forward(values, norm_gain):
    center = values - jnp.mean(values, axis=-1, keepdims=True)
    inverse = lax.rsqrt(jnp.mean(center * center, axis=-1, keepdims=True) + EPSILON)
    normed = center * inverse
    return (normed * norm_gain, normed, inverse)


def norm_backward(grad_out, normed, inverse, norm_gain):
    scaled = grad_out * norm_gain
    return inverse * (
        scaled
        - jnp.mean(scaled, axis=-1, keepdims=True)
        - normed * jnp.mean(scaled * normed, axis=-1, keepdims=True)
    )


def edge_forward(source, dest_proj, sender, target, live_count, out_weight, mesh_count):
    preact = source[sender] + dest_proj[target]
    hidden = jax.nn.silu(preact).astype(jnp.bfloat16)
    message = jnp.dot(hidden, out_weight, preferred_element_type=jnp.float32).astype(jnp.bfloat16)
    live_slots = jnp.arange(sender.shape[0], dtype=jnp.int32) < live_count
    onehot = (
        (target[None, :] == jnp.arange(mesh_count, dtype=jnp.int32)[:, None]) & live_slots[None, :]
    ).astype(jnp.bfloat16)
    gathered = jnp.dot(onehot, message, preferred_element_type=jnp.float32)
    return (gathered, preact, onehot, live_slots)


def edge_backward(
    grad_gathered, preact, onehot, live_slots, sender, target, out_weight, table_rows
):
    grad_message = jnp.where(live_slots[:, None], grad_gathered[target], 0.0).astype(jnp.bfloat16)
    grad_hidden = jnp.dot(grad_message, out_weight.T, preferred_element_type=jnp.float32)
    grad_preact = (grad_hidden * silu_slope(preact)).astype(jnp.bfloat16)
    chooser = (sender[None, :] == jnp.arange(table_rows, dtype=jnp.int32)[:, None]).astype(
        jnp.bfloat16
    )
    grad_source = jnp.dot(chooser, grad_preact, preferred_element_type=jnp.float32)
    grad_dest = jnp.dot(onehot, grad_preact, preferred_element_type=jnp.float32)
    return (grad_source, grad_dest)


def encoder_pass(
    extended,
    mesh_rows,
    sender,
    target,
    live_count,
    source_weight,
    dest_weight,
    out_weight,
    norm_gain,
):
    source = jnp.dot(extended, source_weight, preferred_element_type=jnp.float32)
    dest_proj = jnp.dot(mesh_rows, dest_weight, preferred_element_type=jnp.float32)
    gathered, preact, onehot, live_slots = edge_forward(
        source, dest_proj, sender, target, live_count, out_weight, mesh_rows.shape[0]
    )
    shifted, normed, inverse = norm_forward(gathered, norm_gain)
    updated = (mesh_rows.astype(jnp.float32) + shifted).astype(jnp.bfloat16)
    return (updated, (preact, onehot, live_slots, normed, inverse))


def encoder_backward(
    grad_updated, stored, table_rows, sender, target, dest_weight, out_weight, norm_gain
):
    preact, onehot, live_slots, normed, inverse = stored
    grad_gathered = norm_backward(grad_updated, normed, inverse, norm_gain)
    grad_source, grad_dest = edge_backward(
        grad_gathered, preact, onehot, live_slots, sender, target, out_weight, table_rows
    )
    mesh_grad = grad_updated + jnp.dot(
        grad_dest.astype(jnp.bfloat16), dest_weight.T, preferred_element_type=jnp.float32
    )
    return (mesh_grad, grad_source.astype(jnp.bfloat16))


def process_grads(
    updated,
    coarse_proj,
    sender,
    target,
    live_count,
    cotangent,
    source_weight,
    dest_weight,
    out_weight,
    norm_gain,
):
    local_proj = jnp.dot(updated, source_weight, preferred_element_type=jnp.float32)
    source = jnp.concatenate([local_proj, coarse_proj], axis=0)
    dest_proj = jnp.dot(updated, dest_weight, preferred_element_type=jnp.float32)
    gathered, preact, onehot, live_slots = edge_forward(
        source, dest_proj, sender, target, live_count, out_weight, updated.shape[0]
    )
    unused, normed, inverse = norm_forward(gathered, norm_gain)
    grad_out = cotangent.astype(jnp.float32)
    grad_gathered = norm_backward(grad_out, normed, inverse, norm_gain)
    grad_source, grad_dest = edge_backward(
        grad_gathered, preact, onehot, live_slots, sender, target, out_weight, source.shape[0]
    )
    mesh_count = updated.shape[0]
    grad_local = grad_out + jnp.dot(
        grad_source[:mesh_count].astype(jnp.bfloat16),
        source_weight.T,
        preferred_element_type=jnp.float32,
    )
    grad_local = grad_local + jnp.dot(
        grad_dest.astype(jnp.bfloat16), dest_weight.T, preferred_element_type=jnp.float32
    )
    return (grad_local, grad_source[mesh_count:])


def on_device(
    grid_latent,
    mesh_latent,
    cotangent,
    halo_rows,
    encoder_sender,
    encoder_target,
    encoder_count,
    process_sender,
    process_target,
    process_count,
    encoder_source,
    encoder_dest,
    encoder_output,
    encoder_gain,
    process_source,
    process_dest,
    process_output,
    process_gain,
):
    rim_size = halo_rows.shape[0] // 2
    grid_rows = grid_latent.shape[0]
    outgoing = grid_latent[halo_rows]
    padded = padded_2(outgoing, (("patch", 0),), rim_size)
    extended = jnp.concatenate([grid_latent, padded[:rim_size], padded[3 * rim_size :]], axis=0)
    updated, stored = encoder_pass(
        extended,
        mesh_latent,
        encoder_sender,
        encoder_target,
        encoder_count[0],
        encoder_source,
        encoder_dest,
        encoder_output,
        encoder_gain,
    )
    coarse_rows = mesh_latent.shape[0] // 16
    coarse_proj = jnp.dot(
        lax.all_gather(updated[:coarse_rows], "group", axis=0, tiled=True),
        process_source,
        preferred_element_type=jnp.float32,
    )
    grad_local, grad_coarse = process_grads(
        updated,
        coarse_proj,
        process_sender,
        process_target,
        process_count[0],
        cotangent,
        process_source,
        process_dest,
        process_output,
        process_gain,
    )
    back_weight = process_source.astype(jnp.float32).T
    coarse_grad = lax.psum_scatter(
        jnp.dot(
            grad_coarse,
            back_weight,
            precision=lax.Precision.HIGHEST,
            preferred_element_type=jnp.float32,
        ),
        "group",
        scatter_dimension=0,
        tiled=True,
    )
    grad_updated = grad_local.at[:coarse_rows].add(coarse_grad)
    mesh_grad, source_grads = encoder_backward(
        grad_updated,
        stored,
        extended.shape[0],
        encoder_sender,
        encoder_target,
        encoder_dest,
        encoder_output,
        encoder_gain,
    )
    own_grad = jnp.dot(
        source_grads[:grid_rows], encoder_source.T, preferred_element_type=jnp.float32
    )
    returned = padded_2(source_grads[grid_rows:], (("patch", 0),), rim_size)
    peer_sources = jnp.concatenate([returned[:rim_size], returned[3 * rim_size :]], axis=0)
    from_peers = jnp.dot(peer_sources, encoder_source.T, preferred_element_type=jnp.float32)
    grid_grad = own_grad.at[halo_rows].add(from_peers)
    return (grid_grad.astype(jnp.bfloat16), mesh_grad.astype(jnp.bfloat16))


def solution(mesh):
    return jax.shard_map(
        on_device,
        mesh=mesh,
        in_specs=(
            P(("patch", "group"), None),
            P(("patch", "group"), None),
            P(("patch", "group"), None),
            P(("patch", "group")),
            P(("patch", "group")),
            P(("patch", "group")),
            P(("patch", "group")),
            P(("patch", "group")),
            P(("patch", "group")),
            P(("patch", "group")),
            P(),
            P(),
            P(),
            P(),
            P(),
            P(),
            P(),
            P(),
        ),
        out_specs=(P(("patch", "group"), None), P(("patch", "group"), None)),
        check_vma=False,
    )
```

profile of v0, /device:TPU:1, one launch (start us, length us, event | category | flops | bytes accessed | tf_op | source)
XLA Modules:
  0.0 108.4 jit_solution(11747875148235382991)
XLA Ops:
  7.3 0.8 compare_select_fusion.4
  8.1 0.6 copy-done.13
  8.7 2.3 %gather_fusion = bf16[256,512]{1,0:T(8,128)(2,1)S(1)} fusion(bf16[512,512]{1,0:T(8,128)(2,1)} %param.20, s32[1024]{0:T(1024)S(1)} %pad_clamp_fusion.4), kind=kCustom, calls=%fused_computation | custom fusion | bytes 525312 | tf_op jit(solution)/shard_map/gather | solution.py:162
  11.0 2.6 %collective-permute-start = (bf16[128,512]{1,0:T(8,128)(2,1)S(1)}, bf16[128,512]{1,0:T(8,128)(2,1)S(1)}, u32[]{:S(2)}, u32[]{:S(2)}) collective-permute-start(bf16[128,512]{1,0:T(8,128)(2,1)S(1)} %get-tuple-element.20), channel_id=1, source_target_pairs={{0,4},{4,8},{8,12},{12,16},{16,20},{20,24},{24,28},{28,0},{1,5},{5... | collective-permute-start | bytes 393224 | tf_op jit(solution)/shard_map/ppermute | solution.py:16
  15.5 3.1 %gather_fusion.2 = f32[768,512]{1,0:T(8,128)} fusion(f32[256,512]{1,0:T(8,128)S(1)} %fusion.69, s32[1024]{0:T(1024)S(1)} %pad_clamp_fusion.2), kind=kCustom, calls=%fused_computation.2 | custom fusion | bytes 3148800 | tf_op jit(solution)/shard_map/gather | solution.py:44
  18.6 0.6 fusion.7
  19.2 3.1 %gather_fusion.1 = f32[768,512]{1,0:T(8,128)} fusion(f32[768,512]{1,0:T(8,128)S(1)} %fusion.7, s32[1024]{0:T(1024)S(1)} %pad_clamp_fusion.3), kind=kCustom, calls=%fused_computation.1 | custom fusion | bytes 3148800 | tf_op jit(solution)/shard_map/gather | solution.py:44
  22.3 2.9 %fusion.67 = (f32[256]{0:T(256)S(1)}, f32[256,512]{1,0:T(8,128)S(1)}) fusion(bf16[512,512]{1,0:T(8,128)(2,1)} %param.32, f32[768,512]{1,0:T(8,128)} %gather_fusion.1, f32[768,512]{1,0:T(8,128)} %gather_fusion.2, s32[768]{0:T(1024)S(1)} %copy-done.18, pred[768]{0:T(1024)(128)(4,1)S(1)} %iota_compare_fusion.9), kind=kOutput, calls=%fused_computation.111 | convolution fusion | flops 607256320 | bytes 4199168 | tf_op jit(solution)/shard_map/dot_general | solution.py:51
  25.7 10.7 %all_gather.3 = bf16[64,512]{1,0:T(8,128)(2,1)S(1)} all-gather(bf16[16,512]{1,0:T(8,128)(2,1)S(1)} %slice.72), channel_id=1, replica_groups=mesh['patch'=8,'group'=4] {'group'}, dimensions={0}, use_global_device_ids=true | all-gather | bytes 81920 | tf_op jit(solution)/shard_map/all_gather | solution.py:178
  37.3 3.1 %gather_fusion.3 = f32[768,512]{1,0:T(8,128)} fusion(f32[320,512]{1,0:T(8,128)S(1)} %pad_maximum_fusion, s32[1024]{0:T(1024)S(1)} %pad_clamp_fusion.1), kind=kCustom, calls=%fused_computation.3 | custom fusion | bytes 3148800 | tf_op jit(solution)/shard_map/gather | solution.py:44
  40.4 3.1 %gather_fusion.4 = f32[768,512]{1,0:T(8,128)} fusion(f32[256,512]{1,0:T(8,128)S(1)} %fusion.72, s32[1024]{0:T(1024)S(1)} %pad_clamp_fusion), kind=kCustom, calls=%fused_computation.4 | custom fusion | bytes 3148800 | tf_op jit(solution)/shard_map/gather | solution.py:44
  43.5 2.9 %fusion.68 = (f32[256]{0:T(256)S(1)}, f32[256,512]{1,0:T(8,128)S(1)}) fusion(bf16[512,512]{1,0:T(8,128)(2,1)} %param.36, f32[768,512]{1,0:T(8,128)} %gather_fusion.3, f32[768,512]{1,0:T(8,128)} %gather_fusion.4, s32[768]{0:T(1024)S(1)} %copy-done.10, pred[768]{0:T(1024)(128)(4,1)S(1)} %iota_compare_fusion.8), kind=kOutput, calls=%fused_computation.112 | convolution fusion | flops 607256320 | bytes 4199168 | tf_op jit(solution)/shard_map/dot_general | solution.py:51
  47.1 3.3 %gather_fusion.5 = bf16[768,512]{1,0:T(8,128)(2,1)} fusion(bf16[256,512]{1,0:T(8,128)(2,1)S(1)} %fusion.33, s32[1024]{0:T(1024)S(1)} %pad_clamp_fusion), kind=kCustom, calls=%fused_computation.5 | custom fusion | bytes 1575936 | tf_op jit(solution)/shard_map/gather | solution.py:58
  50.5 3.2 %multiply_convert_fusion.1 = bf16[768,512]{1,0:T(8,128)(2,1)S(1)} fusion(bf16[512,512]{1,0:T(8,128)(2,1)} %param.36, bf16[768,512]{1,0:T(8,128)(2,1)} %gather_fusion.5, pred[768]{0:T(1024)(128)(4,1)S(1)} %iota_compare_fusion.8, f32[768,512]{1,0:T(8,128)} %gather_fusion.3, f32[768,512]{1,0:T(8,128)} %gather_fusion.4), kind=kOutput, calls=%fused_computation.12 | convolution fusion | flops 406978560 | bytes 5243648 | tf_op jit(solution)/shard_map/dot_general | solution.py:59
  53.7 0.9 copy-done.6
  54.6 0.4 fusion.6
  55.0 1.3 %fusion.54 = f32[64,512]{1,0:T(8,128)} fusion(bf16[512,512]{1,0:T(8,128)(2,1)S(1)} %copy-done.1, f32[320,512]{1,0:T(8,128)S(1)} %fusion.6), kind=kOutput, calls=%fused_computation.79 | convolution fusion | flops 201326592 | bytes 786432 | tf_op jit(solution)/shard_map/dot_general | solution.py:196
  56.3 0.3 convolution_add_fusion.2
  56.6 1.7 %convolution_add_fusion.1 = f32[256,512]{1,0:T(8,128)S(1)} fusion(f32[256,512]{1,0:T(8,128)S(1)} %convolution_add_fusion.2, bf16[512,512]{1,0:T(8,128)(2,1)S(1)} %copy-done.4, bf16[768,512]{1,0:T(8,128)(2,1)} %copy-done.6, s32[768]{0:T(1024)S(1)} %copy-done.10, pred[768]{0:T(1024)(128)(4,1)} %copy-done.22), kind=kOutput, calls=%fused_computation.24 | convolution fusion | flops 336199680 | bytes 2363136 | tf_op jit(solution)/shard_map/dot_general | solution.py:134
  58.4 19.3 %reduce-scatter.2.cloned.1.call-done = f32[16,512]{1,0:T(8,128)} async-done(((f32[64,512]{1,0:T(8,128)}), f32[16,512]{1,0:T(8,128)}) %reduce-scatter.2.cloned.1.call-update) | async-done | bytes 32784 | tf_op jit(solution)/shard_map/reduce_scatter | solution.py:195
  77.7 0.8 fusion.56
  79.0 2.7 %gather_fusion.6 = bf16[768,512]{1,0:T(8,128)(2,1)S(1)} fusion(bf16[256,512]{1,0:T(8,128)(2,1)S(1)} %subtract_multiply_fusion, s32[1024]{0:T(1024)S(1)} %pad_clamp_fusion.2), kind=kCustom, calls=%fused_computation.6 | custom fusion | bytes 1575936 | tf_op jit(solution)/shard_map/gather | solution.py:58
  81.7 3.7 %multiply_convert_fusion = bf16[768,512]{1,0:T(8,128)(2,1)} fusion(bf16[512,512]{1,0:T(8,128)(2,1)S(1)} %copy-done.23, bf16[768,512]{1,0:T(8,128)(2,1)S(1)} %gather_fusion.6, pred[768]{0:T(1024)(128)(4,1)S(1)} %copy-done.25, f32[768,512]{1,0:T(8,128)} %gather_fusion.1, f32[768,512]{1,0:T(8,128)} %gather_fusion.2), kind=kOutput, calls=%fused_computation.10 | convolution fusion | flops 406978560 | bytes 5243648 | tf_op jit(solution)/shard_map/dot_general | solution.py:59
  85.5 2.5 %fusion.4 = bf16[256,512]{1,0:T(8,128)(2,1)} fusion(f32[256,512]{1,0:T(8,128)S(1)} %fusion.56, bf16[512,512]{1,0:T(8,128)(2,1)S(1)} %copy-done.8, bf16[768,512]{1,0:T(8,128)(2,1)} %multiply_convert_fusion, s32[768]{0:T(1024)S(1)} %copy-done.19, pred[768]{0:T(1024)(128)(4,1)S(1)} %copy-done.25), kind=kOutput, calls=%fused_computation.26 | convolution fusion | flops 336330752 | bytes 2100992 | tf_op jit(solution)/shard_map/dot_general | solution.py:98
  88.0 0.8 fusion.1
  88.8 4.1 %collective-permute-start.2 = (bf16[128,512]{1,0:T(8,128)(2,1)S(1)}, bf16[128,512]{1,0:T(8,128)(2,1)S(1)}, u32[]{:S(2)}, u32[]{:S(2)}) collective-permute-start(bf16[128,512]{1,0:T(8,128)(2,1)S(1)} %get-tuple-element.18), channel_id=1, source_target_pairs={{0,4},{4,8},{8,12},{12,16},{16,20},{20,24},{24,28},{28,0},{1,5},{5... | collective-permute-start | bytes 393224 | tf_op jit(solution)/shard_map/ppermute | solution.py:16
  92.9 0.5 fusion.35
  93.4 1.5 %collective-permute-done.2 = bf16[128,512]{1,0:T(8,128)(2,1)S(1)} collective-permute-done((bf16[128,512]{1,0:T(8,128)(2,1)S(1)}, bf16[128,512]{1,0:T(8,128)(2,1)S(1)}, u32[]{:S(2)}, u32[]{:S(2)}) %collective-permute-start.2) | collective-permute-done | bytes 131104 | tf_op jit(solution)/shard_map/ppermute | solution.py:16
  94.9 3.0 %collective-permute-done.3 = bf16[128,512]{1,0:T(8,128)(2,1)S(1)} collective-permute-done((bf16[128,512]{1,0:T(8,128)(2,1)S(1)}, bf16[128,512]{1,0:T(8,128)(2,1)S(1)}, u32[]{:S(2)}, u32[]{:S(2)}) %collective-permute-start.3) | collective-permute-done | bytes 131104 | tf_op jit(solution)/shard_map/ppermute | solution.py:17
  97.9 0.3 fusion.50
  98.2 2.5 %scatter_fusion = f32[512,512]{1,0:T(8,128)S(1)} fusion(f32[512,512]{1,0:T(8,128)S(1)} %fusion.35, s32[256]{0:T(256)S(1)} %copy-done.14, f32[256,512]{1,0:T(8,128)S(1)} %fusion.50), kind=kCustom, calls=%fused_computation.7 | custom fusion | flops 131072 | bytes 1573888 | tf_op jit(solution)/shard_map/scatter-add | solution.py:223
  100.7 0.9 convert_element_type.67
  (91 shorter events, 3.0 us)
Async XLA Ops:
  7.2 11.5 %copy-start = (bf16[512,512]{1,0:T(8,128)(2,1)S(1)}, bf16[512,512]{1,0:T(8,128)(2,1)}, u32[]{:S(2)}) copy-start(bf16[512,512]{1,0:T(8,128)(2,1)} %param.30) | copy-start | bytes 1572868
  7.2 7.8 %copy-start.20 = (s32[768]{0:T(1024)S(1)}, s32[768]{0:T(1024)}, u32[]{:S(2)}) copy-start(s32[768]{0:T(1024)} %param.24) | copy-start | bytes 9220
  7.2 7.8 %copy-start.16 = (s32[768]{0:T(1024)S(1)}, s32[768]{0:T(1024)}, u32[]{:S(2)}) copy-start(s32[768]{0:T(1024)} %param.27) | copy-start | bytes 9220
  7.2 7.9 %copy-start.18 = (s32[768]{0:T(1024)S(1)}, s32[768]{0:T(1024)}, u32[]{:S(2)}) copy-start(s32[768]{0:T(1024)} %param.25) | copy-start | bytes 9220
  7.2 7.9 %copy-start.10 = (s32[768]{0:T(1024)S(1)}, s32[768]{0:T(1024)}, u32[]{:S(2)}) copy-start(s32[768]{0:T(1024)} %param.28) | copy-start | bytes 9220
  7.2 7.9 %copy-start.7 = (bf16[512,512]{1,0:T(8,128)(2,1)S(1)}, bf16[512,512]{1,0:T(8,128)(2,1)}, u32[]{:S(2)}) copy-start(bf16[512,512]{1,0:T(8,128)(2,1)} %param.31) | copy-start | bytes 1572868
  7.2 7.9 %copy-start.5 = (bf16[256,512]{1,0:T(8,128)(2,1)S(1)}, bf16[256,512]{1,0:T(8,128)(2,1)}, u32[]{:S(2)}) copy-start(bf16[256,512]{1,0:T(8,128)(2,1)} %param.21) | copy-start | bytes 786436
  7.2 70.4 %reduce-scatter.2.cloned.1.call-start = ((), (), s32[]{:S(2)}) async-start(), calls=%async_computation.1 | async-start | bytes 163840 | tf_op jit(solution)/shard_map/reduce_scatter | solution.py:195
  8.1 0.6 copy-start.13
  11.0 7.6 %collective-permute-start = (bf16[128,512]{1,0:T(8,128)(2,1)S(1)}, bf16[128,512]{1,0:T(8,128)(2,1)S(1)}, u32[]{:S(2)}, u32[]{:S(2)}) collective-permute-start(bf16[128,512]{1,0:T(8,128)(2,1)S(1)} %get-tuple-element.20), channel_id=1, source_target_pairs={{0,4},{4,8},{8,12},{12,16},{16,20},{20,24},{24,28},{28,0},{1,5},{5... | collective-permute-start | bytes 393224 | tf_op jit(solution)/shard_map/ppermute | solution.py:16
  13.7 5.0 %collective-permute-start.1 = (bf16[128,512]{1,0:T(8,128)(2,1)S(1)}, bf16[128,512]{1,0:T(8,128)(2,1)S(1)}, u32[]{:S(2)}, u32[]{:S(2)}) collective-permute-start(bf16[128,512]{1,0:T(8,128)(2,1)S(1)} %get-tuple-element.21), channel_id=1, source_target_pairs={{4,0},{8,4},{12,8},{16,12},{20,16},{24,20},{28,24},{0,28},{5,1},{9... | collective-permute-start | bytes 393224 | tf_op jit(solution)/shard_map/ppermute | solution.py:17
  15.0 7.3 %copy-start.24 = (pred[768]{0:T(1024)(128)(4,1)}, pred[768]{0:T(1024)(128)(4,1)S(1)}, u32[]{:S(2)}) copy-start(pred[768]{0:T(1024)(128)(4,1)S(1)} %iota_compare_fusion.9) | copy-start | bytes 2308
  15.4 35.0 %copy-start.22 = (pred[768]{0:T(1024)(128)(4,1)}, pred[768]{0:T(1024)(128)(4,1)S(1)}, u32[]{:S(2)}) copy-start(pred[768]{0:T(1024)(128)(4,1)S(1)} %iota_compare_fusion.8) | copy-start | bytes 2308
  15.5 3.2 %copy-start.2 = (bf16[512,512]{1,0:T(8,128)(2,1)S(1)}, bf16[512,512]{1,0:T(8,128)(2,1)}, u32[]{:S(2)}) copy-start(bf16[512,512]{1,0:T(8,128)(2,1)} %param.20) | copy-start | bytes 1572868
  22.3 3.1 %copy-start.9 = (f32[512]{0:T(512)S(1)}, f32[512]{0:T(512)}, u32[]{:S(2)}) copy-start(f32[512]{0:T(512)} %param.33) | copy-start | bytes 6148
  25.2 11.2 %copy-start.1 = (bf16[512,512]{1,0:T(8,128)(2,1)S(1)}, bf16[512,512]{1,0:T(8,128)(2,1)}, u32[]{:S(2)}) copy-start(bf16[512,512]{1,0:T(8,128)(2,1)} %param.34) | copy-start | bytes 1572868
  25.4 11.5 %copy-start.11 = (f32[256]{0:T(256)}, f32[256]{0:T(256)S(1)}, u32[]{:S(2)}) copy-start(f32[256]{0:T(256)S(1)} %add_rsqrt_fusion.1) | copy-start | bytes 3076
  25.5 11.5 %copy-start.4 = (bf16[512,512]{1,0:T(8,128)(2,1)S(1)}, bf16[512,512]{1,0:T(8,128)(2,1)}, u32[]{:S(2)}) copy-start(bf16[512,512]{1,0:T(8,128)(2,1)} %param.35) | copy-start | bytes 1572868
  43.5 3.2 %copy-start.3 = (bf16[256,512]{1,0:T(8,128)(2,1)S(1)}, bf16[256,512]{1,0:T(8,128)(2,1)}, u32[]{:S(2)}) copy-start(bf16[256,512]{1,0:T(8,128)(2,1)} %param.22) | copy-start | bytes 786436
  43.5 3.2 %copy-start.15 = (f32[512]{0:T(512)S(1)}, f32[512]{0:T(512)}, u32[]{:S(2)}) copy-start(f32[512]{0:T(512)} %param.37) | copy-start | bytes 6148
  50.5 4.1 %copy-start.17 = (s32[768]{0:T(1024)S(1)}, s32[768]{0:T(1024)}, u32[]{:S(2)}) copy-start(s32[768]{0:T(1024)} %param.27) | copy-start | bytes 9220
  53.7 0.9 copy-start.6
  56.6 21.9 %copy-start.12 = (f32[256]{0:T(256)S(1)}, f32[256]{0:T(256)}, u32[]{:S(2)}) copy-start(f32[256]{0:T(256)} %copy-done.11) | copy-start | bytes 3076
  78.9 2.7 %copy-start.23 = (bf16[512,512]{1,0:T(8,128)(2,1)S(1)}, bf16[512,512]{1,0:T(8,128)(2,1)}, u32[]{:S(2)}) copy-start(bf16[512,512]{1,0:T(8,128)(2,1)} %param.32) | copy-start | bytes 1572868
  79.0 2.7 %copy-start.25 = (pred[768]{0:T(1024)(128)(4,1)S(1)}, pred[768]{0:T(1024)(128)(4,1)}, u32[]{:S(2)}) copy-start(pred[768]{0:T(1024)(128)(4,1)} %copy-done.24) | copy-start | bytes 2308
  81.7 3.8 %copy-start.8 = (bf16[512,512]{1,0:T(8,128)(2,1)S(1)}, bf16[512,512]{1,0:T(8,128)(2,1)}, u32[]{:S(2)}) copy-start(bf16[512,512]{1,0:T(8,128)(2,1)} %param.31) | copy-start | bytes 1572868
  81.7 3.8 %copy-start.19 = (s32[768]{0:T(1024)S(1)}, s32[768]{0:T(1024)}, u32[]{:S(2)}) copy-start(s32[768]{0:T(1024)} %param.25) | copy-start | bytes 9220
  85.5 2.5 %copy-start.21 = (s32[768]{0:T(1024)S(1)}, s32[768]{0:T(1024)}, u32[]{:S(2)}) copy-start(s32[768]{0:T(1024)} %param.24) | copy-start | bytes 9220
  85.5 2.5 %copy-start.26 = (bf16[768,512]{1,0:T(8,128)(2,1)S(1)}, bf16[768,512]{1,0:T(8,128)(2,1)}, u32[]{:S(2)}) copy-start(bf16[768,512]{1,0:T(8,128)(2,1)} %multiply_convert_fusion) | copy-start | bytes 2359300
  88.8 6.1 %collective-permute-start.2 = (bf16[128,512]{1,0:T(8,128)(2,1)S(1)}, bf16[128,512]{1,0:T(8,128)(2,1)S(1)}, u32[]{:S(2)}, u32[]{:S(2)}) collective-permute-start(bf16[128,512]{1,0:T(8,128)(2,1)S(1)} %get-tuple-element.18), channel_id=1, source_target_pairs={{0,4},{4,8},{8,12},{12,16},{16,20},{20,24},{24,28},{28,0},{1,5},{5... | collective-permute-start | bytes 393224 | tf_op jit(solution)/shard_map/ppermute | solution.py:16
  92.9 5.3 %copy-start.14 = (s32[256]{0:T(256)S(1)}, s32[256]{0:T(256)}, u32[]{:S(2)}) copy-start(s32[256]{0:T(256)} %copy-done.13) | copy-start | bytes 3076
  92.9 4.9 %collective-permute-start.3 = (bf16[128,512]{1,0:T(8,128)(2,1)S(1)}, bf16[128,512]{1,0:T(8,128)(2,1)S(1)}, u32[]{:S(2)}, u32[]{:S(2)}) collective-permute-start(bf16[128,512]{1,0:T(8,128)(2,1)S(1)} %get-tuple-element.19), channel_id=1, source_target_pairs={{4,0},{8,4},{12,8},{16,12},{20,16},{24,20},{28,24},{0,28},{5,1},{9... | collective-permute-start | bytes 393224 | tf_op jit(solution)/shard_map/ppermute | solution.py:17
Sparse Core Ops, SparseCore 0:
  56.8 20.8 reduce-scatter.1
where the time goes:
time: 109 us; the launch traced here: 108 us
  waiting for transfers between devices  23.8 us (22%)
  local copies, waits for them, and re-layouts  22.4 us (21%)
  matrix products  22.2 us (20%)
  between operations  15.9 us (15%)
  blocking collectives  10.7 us (10%)
  starting transfers between devices  6.83 us (6%)
  other arithmetic  6.52 us (6%)
    reduce_scatter x1, waiting for transfers between devices, on_device(): lax.psum_scatter(jnp.dot(grad_coarse, back_weight, precision=lax.Precisio...  19.3 us
    gather x4, local copies, waits for them, and re-layouts, edge_forward(): preact = source[sender] + dest_proj[target]  12.5 us
    all_gather x1, blocking collectives, on_device(): lax.all_gather(updated[:coarse_rows], 'group', axis=0, tiled=True)  10.7 us
    dot_general x2, matrix products, edge_backward(): jnp.dot(grad_message, out_weight.T, preferred_element_type=jnp.float32)  6.96 us
    ppermute x2, starting transfers between devices, padded_2(): before = lax.ppermute(last, axis, up)  6.78 us
    gather x2, local copies, waits for them, and re-layouts, edge_backward(): grad_gathered[target]  6 us
    dot_general x2, matrix products, edge_forward(): gathered = jnp.dot(onehot, message, preferred_element_type=jnp.float32)  5.79 us
    ppermute x2, waiting for transfers between devices, padded_2(): after = lax.ppermute(initial, axis, down)  3.03 us
  transfers between devices with their start and end apart: 5, of which 3 were waited for; matrix products, arithmetic and copies ran while one was open for 5% of the time, Pallas kernels for 0%

commit v1 on v0

--- a/solution.py
+++ b/solution.py
@@ -4,6 +4,28 @@
 from jax.sharding import PartitionSpec as P
 
 EPSILON = 1e-05
+
+
+def laid_out(blocks, dim):
+    blocks = jnp.moveaxis(blocks, 0, dim)
+    dims = blocks.shape
+    return blocks.reshape(*dims[:dim], dims[dim] * dims[dim + 1], *dims[dim + 2 :])
+
+
+def collect(array, axis, dim):
+    size = lax.axis_size(axis)
+    pairs = [(i, (i + 1) % size) for i in range(size)]
+    back = [(b, a) for a, b in pairs]
+    lower, upper = ([], [])
+    for step in range(size - 1):
+        if step % 2 == 0:
+            lower.append(lax.ppermute(lower[-1] if lower else array, axis, pairs))
+        else:
+            upper.append(lax.ppermute(upper[-1] if upper else array, axis, back))
+    pieces = jnp.stack([*lower[::-1], array, *upper])
+    shift = lax.axis_index(axis) - len(lower)
+    pieces = pieces[(jnp.arange(size) - shift) % size]
+    return laid_out(pieces, dim)
 
 
 def padded_2(x, sides, width):
@@ -175,7 +197,7 @@
     )
     coarse_rows = mesh_latent.shape[0] // 16
     coarse_proj = jnp.dot(
-        lax.all_gather(updated[:coarse_rows], "group", axis=0, tiled=True),
+        collect(updated[:coarse_rows], "group", 0),
         process_source,
         preferred_element_type=jnp.float32,
     )

time: 109 us -> 105 us (0.963)
  blocking collectives: 10.7 us -> 0 us
  starting transfers between devices: 6.83 us -> 10.2 us
  waiting for transfers between devices: 23.8 us -> 27 us
    all_gather x1 -> x0, blocking collectives: 10.7 us -> none  [on_device(): lax.all_gather(updated[:coarse_rows], 'group', axis=0, tiled=True)]
    ppermute x0 -> x3, waiting for transfers between devices: none -> 5.02 us  [the longest x2 5.02 us: collect(): lower.append(lax.ppermute(lower[-1] if lower else array, axis, pairs))]
    ppermute x0 -> x3, starting transfers between devices: none -> 3.37 us  [the longest x1 3.36 us: collect(): upper.append(lax.ppermute(upper[-1] if upper else array, axis, back))]
    reduce_scatter x1, waiting for transfers between devices: 19.3 us -> 17.4 us  [on_device(): lax.psum_scatter(jnp.dot(grad_coarse, back_weight, precision=lax.Precisio...]
  transfers between devices with their start and end apart: 5 -> 8, of which waited for: 3 -> 5; matrix products, arithmetic and copies ran while one was open for 5% -> 9% of each run, Pallas kernels for 0% -> 0%
where the time goes in v1:
time: 105 us
  waiting for transfers between devices  27 us (26%)
  local copies, waits for them, and re-layouts  23 us (22%)
  matrix products  22.3 us (21%)
  between operations  15.9 us (15%)
  starting transfers between devices  10.2 us (10%)
  other arithmetic  6.55 us (6%)
    reduce_scatter x1, waiting for transfers between devices, on_device(): lax.psum_scatter(jnp.dot(grad_coarse, back_weight, precision=lax.Precisio...  17.4 us
    gather x4, local copies, waits for them, and re-layouts, edge_forward(): preact = source[sender] + dest_proj[target]  12.5 us
    dot_general x2, matrix products, edge_backward(): jnp.dot(grad_message, out_weight.T, preferred_element_type=jnp.float32)  6.96 us
    ppermute x2, starting transfers between devices, padded_2(): before = lax.ppermute(last, axis, up)  6.84 us
    gather x2, local copies, waits for them, and re-layouts, edge_backward(): grad_gathered[target]  6.02 us
    dot_general x2, matrix products, edge_forward(): gathered = jnp.dot(onehot, message, preferred_element_type=jnp.float32)  5.8 us
    ppermute x2, waiting for transfers between devices, collect(): lower.append(lax.ppermute(lower[-1] if lower else array, axis, pairs))  5.02 us
    ppermute x1, starting transfers between devices, collect(): upper.append(lax.ppermute(upper[-1] if upper else array, axis, back))  3.36 us
  transfers between devices with their start and end apart: 8, of which 5 were waited for; matrix products, arithmetic and copies ran while one was open for 9% of the time, Pallas kernels for 0%

profile of v1, /device:TPU:1, one launch (start us, length us, event | category | flops | bytes accessed | tf_op | source)
XLA Modules:
  0.0 105.0 jit_solution(16233820574141950155)
XLA Ops:
  7.3 0.8 compare_select_fusion.4
  8.1 0.6 copy-done.13
  8.7 2.3 %gather_fusion = bf16[256,512]{1,0:T(8,128)(2,1)S(1)} fusion(bf16[512,512]{1,0:T(8,128)(2,1)} %param.20, s32[1024]{0:T(1024)S(1)} %pad_clamp_fusion.5), kind=kCustom, calls=%fused_computation | custom fusion | bytes 525312 | tf_op jit(solution)/shard_map/gather | solution.py:184
  11.0 2.6 %collective-permute-start = (bf16[128,512]{1,0:T(8,128)(2,1)S(1)}, bf16[128,512]{1,0:T(8,128)(2,1)S(1)}, u32[]{:S(2)}, u32[]{:S(2)}) collective-permute-start(bf16[128,512]{1,0:T(8,128)(2,1)S(1)} %get-tuple-element.22), channel_id=1, source_target_pairs={{0,4},{4,8},{8,12},{12,16},{16,20},{20,24},{24,28},{28,0},{1,5},{5... | collective-permute-start | bytes 393224 | tf_op jit(solution)/shard_map/ppermute | solution.py:38
  15.5 3.1 %gather_fusion.2 = f32[768,512]{1,0:T(8,128)} fusion(f32[256,512]{1,0:T(8,128)S(1)} %fusion.71, s32[1024]{0:T(1024)S(1)} %pad_clamp_fusion.3), kind=kCustom, calls=%fused_computation.2 | custom fusion | bytes 3148800 | tf_op jit(solution)/shard_map/gather | solution.py:66
  18.7 0.6 fusion.7
  19.3 3.1 %gather_fusion.1 = f32[768,512]{1,0:T(8,128)} fusion(f32[768,512]{1,0:T(8,128)S(1)} %fusion.7, s32[1024]{0:T(1024)S(1)} %pad_clamp_fusion.4), kind=kCustom, calls=%fused_computation.1 | custom fusion | bytes 3148800 | tf_op jit(solution)/shard_map/gather | solution.py:66
  22.4 2.9 %fusion.69 = (f32[256]{0:T(256)S(1)}, f32[256,512]{1,0:T(8,128)S(1)}) fusion(bf16[512,512]{1,0:T(8,128)(2,1)} %param.32, f32[768,512]{1,0:T(8,128)} %gather_fusion.1, f32[768,512]{1,0:T(8,128)} %gather_fusion.2, s32[768]{0:T(1024)S(1)} %copy-done.18, pred[768]{0:T(1024)(128)(4,1)S(1)} %iota_compare_fusion.9), kind=kOutput, calls=%fused_computation.121 | convolution fusion | flops 607256320 | bytes 4199168 | tf_op jit(solution)/shard_map/dot_general | solution.py:73
  25.7 3.4 %collective-permute-start.4 = (bf16[16,512]{1,0:T(8,128)(2,1)S(1)}, bf16[16,512]{1,0:T(8,128)(2,1)S(1)}, u32[]{:S(2)}, u32[]{:S(2)}) collective-permute-start(bf16[16,512]{1,0:T(8,128)(2,1)S(1)} %get-tuple-element.21), channel_id=1, source_target_pairs={{1,0},{2,1},{3,2},{0,3},{5,4},{6,5},{7,6},{4,7},{9,8},{10,9},{11,1... | collective-permute-start | bytes 49160 | tf_op jit(solution)/shard_map/ppermute | solution.py:24
  29.4 4.1 %collective-permute-done.2 = bf16[16,512]{1,0:T(8,128)(2,1)S(1)} collective-permute-done((bf16[16,512]{1,0:T(8,128)(2,1)S(1)}, bf16[16,512]{1,0:T(8,128)(2,1)S(1)}, u32[]{:S(2)}, u32[]{:S(2)}) %collective-permute-start.2) | collective-permute-done | bytes 16416 | tf_op jit(solution)/shard_map/ppermute | solution.py:22
  33.8 3.1 %gather_fusion.5 = f32[768,512]{1,0:T(8,128)} fusion(f32[256,512]{1,0:T(8,128)S(1)} %fusion.74, s32[1024]{0:T(1024)S(1)} %pad_clamp_fusion), kind=kCustom, calls=%fused_computation.5 | custom fusion | bytes 3148800 | tf_op jit(solution)/shard_map/gather | solution.py:66
  36.9 0.9 collective-permute-done.3
  37.9 0.6 gather_fusion.3
  38.7 3.1 %gather_fusion.4 = f32[768,512]{1,0:T(8,128)} fusion(f32[320,512]{1,0:T(8,128)S(1)} %pad_maximum_fusion, s32[1024]{0:T(1024)S(1)} %pad_clamp_fusion.1), kind=kCustom, calls=%fused_computation.4 | custom fusion | bytes 3148800 | tf_op jit(solution)/shard_map/gather | solution.py:66
  41.8 2.9 %fusion.70 = (f32[256]{0:T(256)S(1)}, f32[256,512]{1,0:T(8,128)S(1)}) fusion(bf16[512,512]{1,0:T(8,128)(2,1)} %param.36, f32[768,512]{1,0:T(8,128)} %gather_fusion.4, f32[768,512]{1,0:T(8,128)} %gather_fusion.5, s32[768]{0:T(1024)S(1)} %copy-done.10, pred[768]{0:T(1024)(128)(4,1)S(1)} %iota_compare_fusion.8), kind=kOutput, calls=%fused_computation.122 | convolution fusion | flops 607256320 | bytes 4199168 | tf_op jit(solution)/shard_map/dot_general | solution.py:73
  45.5 3.3 %gather_fusion.6 = bf16[768,512]{1,0:T(8,128)(2,1)} fusion(bf16[256,512]{1,0:T(8,128)(2,1)S(1)} %fusion.33, s32[1024]{0:T(1024)S(1)} %pad_clamp_fusion), kind=kCustom, calls=%fused_computation.6 | custom fusion | bytes 1575936 | tf_op jit(solution)/shard_map/gather | solution.py:80
  48.8 3.2 %multiply_convert_fusion.1 = bf16[768,512]{1,0:T(8,128)(2,1)S(1)} fusion(bf16[512,512]{1,0:T(8,128)(2,1)} %param.36, bf16[768,512]{1,0:T(8,128)(2,1)} %gather_fusion.6, pred[768]{0:T(1024)(128)(4,1)S(1)} %iota_compare_fusion.8, f32[768,512]{1,0:T(8,128)} %gather_fusion.4, f32[768,512]{1,0:T(8,128)} %gather_fusion.5), kind=kOutput, calls=%fused_computation.13 | convolution fusion | flops 406978560 | bytes 5243648 | tf_op jit(solution)/shard_map/dot_general | solution.py:81
  52.0 0.9 copy-done.6
  53.4 1.3 %fusion.54 = f32[64,512]{1,0:T(8,128)} fusion(bf16[512,512]{1,0:T(8,128)(2,1)S(1)} %copy-done.1, f32[320,512]{1,0:T(8,128)S(1)} %fusion.6), kind=kOutput, calls=%fused_computation.80 | convolution fusion | flops 201326592 | bytes 786432 | tf_op jit(solution)/shard_map/dot_general | solution.py:218
  55.0 1.7 %convolution_add_fusion.1 = f32[256,512]{1,0:T(8,128)S(1)} fusion(f32[256,512]{1,0:T(8,128)S(1)} %convolution_add_fusion.2, bf16[512,512]{1,0:T(8,128)(2,1)S(1)} %copy-done.4, bf16[768,512]{1,0:T(8,128)(2,1)} %copy-done.6, s32[768]{0:T(1024)S(1)} %copy-done.10, pred[768]{0:T(1024)(128)(4,1)} %copy-done.22), kind=kOutput, calls=%fused_computation.25 | convolution fusion | flops 336199680 | bytes 2363136 | tf_op jit(solution)/shard_map/dot_general | solution.py:156
  56.7 17.4 %reduce-scatter.2.cloned.1.call-done = f32[16,512]{1,0:T(8,128)} async-done(((f32[64,512]{1,0:T(8,128)}), f32[16,512]{1,0:T(8,128)}) %reduce-scatter.2.cloned.1.call-update) | async-done | bytes 32784 | tf_op jit(solution)/shard_map/reduce_scatter | solution.py:217
  74.2 0.8 fusion.56
  75.4 2.7 %gather_fusion.7 = bf16[768,512]{1,0:T(8,128)(2,1)S(1)} fusion(bf16[256,512]{1,0:T(8,128)(2,1)S(1)} %subtract_multiply_fusion, s32[1024]{0:T(1024)S(1)} %pad_clamp_fusion.3), kind=kCustom, calls=%fused_computation.7 | custom fusion | bytes 1575936 | tf_op jit(solution)/shard_map/gather | solution.py:80
  78.2 3.8 %multiply_convert_fusion = bf16[768,512]{1,0:T(8,128)(2,1)} fusion(bf16[512,512]{1,0:T(8,128)(2,1)S(1)} %copy-done.23, bf16[768,512]{1,0:T(8,128)(2,1)S(1)} %gather_fusion.7, pred[768]{0:T(1024)(128)(4,1)S(1)} %copy-done.25, f32[768,512]{1,0:T(8,128)} %gather_fusion.1, f32[768,512]{1,0:T(8,128)} %gather_fusion.2), kind=kOutput, calls=%fused_computation.11 | convolution fusion | flops 406978560 | bytes 5243648 | tf_op jit(solution)/shard_map/dot_general | solution.py:81
  81.9 2.5 %fusion.4 = bf16[256,512]{1,0:T(8,128)(2,1)} fusion(f32[256,512]{1,0:T(8,128)S(1)} %fusion.56, bf16[512,512]{1,0:T(8,128)(2,1)S(1)} %copy-done.8, bf16[768,512]{1,0:T(8,128)(2,1)} %multiply_convert_fusion, s32[768]{0:T(1024)S(1)} %copy-done.19, pred[768]{0:T(1024)(128)(4,1)S(1)} %copy-done.25), kind=kOutput, calls=%fused_computation.27 | convolution fusion | flops 336330752 | bytes 2100992 | tf_op jit(solution)/shard_map/dot_general | solution.py:120
  84.4 0.8 fusion.1
  85.3 4.2 %collective-permute-start.5 = (bf16[128,512]{1,0:T(8,128)(2,1)S(1)}, bf16[128,512]{1,0:T(8,128)(2,1)S(1)}, u32[]{:S(2)}, u32[]{:S(2)}) collective-permute-start(bf16[128,512]{1,0:T(8,128)(2,1)S(1)} %get-tuple-element.18), channel_id=1, source_target_pairs={{0,4},{4,8},{8,12},{12,16},{16,20},{20,24},{24,28},{28,0},{1,5},{5... | collective-permute-start | bytes 393224 | tf_op jit(solution)/shard_map/ppermute | solution.py:38
  89.5 0.5 fusion.35
  89.9 1.5 %collective-permute-done.5 = bf16[128,512]{1,0:T(8,128)(2,1)S(1)} collective-permute-done((bf16[128,512]{1,0:T(8,128)(2,1)S(1)}, bf16[128,512]{1,0:T(8,128)(2,1)S(1)}, u32[]{:S(2)}, u32[]{:S(2)}) %collective-permute-start.5) | collective-permute-done | bytes 131104 | tf_op jit(solution)/shard_map/ppermute | solution.py:38
  91.4 3.0 %collective-permute-done.6 = bf16[128,512]{1,0:T(8,128)(2,1)S(1)} collective-permute-done((bf16[128,512]{1,0:T(8,128)(2,1)S(1)}, bf16[128,512]{1,0:T(8,128)(2,1)S(1)}, u32[]{:S(2)}, u32[]{:S(2)}) %collective-permute-start.6) | collective-permute-done | bytes 131104 | tf_op jit(solution)/shard_map/ppermute | solution.py:39
  94.8 2.5 %scatter_fusion = f32[512,512]{1,0:T(8,128)S(1)} fusion(f32[512,512]{1,0:T(8,128)S(1)} %fusion.35, s32[256]{0:T(256)S(1)} %copy-done.14, f32[256,512]{1,0:T(8,128)S(1)} %fusion.50), kind=kCustom, calls=%fused_computation.8 | custom fusion | flops 131072 | bytes 1573888 | tf_op jit(solution)/shard_map/scatter-add | solution.py:245
  97.3 0.9 convert_element_type.67
  (100 shorter events, 4.1 us)
Async XLA Ops:
  7.2 11.5 %copy-start = (bf16[512,512]{1,0:T(8,128)(2,1)S(1)}, bf16[512,512]{1,0:T(8,128)(2,1)}, u32[]{:S(2)}) copy-start(bf16[512,512]{1,0:T(8,128)(2,1)} %param.30) | copy-start | bytes 1572868
  7.2 7.8 %copy-start.20 = (s32[768]{0:T(1024)S(1)}, s32[768]{0:T(1024)}, u32[]{:S(2)}) copy-start(s32[768]{0:T(1024)} %param.24) | copy-start | bytes 9220
  7.2 7.9 %copy-start.16 = (s32[768]{0:T(1024)S(1)}, s32[768]{0:T(1024)}, u32[]{:S(2)}) copy-start(s32[768]{0:T(1024)} %param.27) | copy-start | bytes 9220
  7.2 7.9 %copy-start.18 = (s32[768]{0:T(1024)S(1)}, s32[768]{0:T(1024)}, u32[]{:S(2)}) copy-start(s32[768]{0:T(1024)} %param.25) | copy-start | bytes 9220
  7.2 7.9 %copy-start.10 = (s32[768]{0:T(1024)S(1)}, s32[768]{0:T(1024)}, u32[]{:S(2)}) copy-start(s32[768]{0:T(1024)} %param.28) | copy-start | bytes 9220
  7.2 7.9 %copy-start.7 = (bf16[512,512]{1,0:T(8,128)(2,1)S(1)}, bf16[512,512]{1,0:T(8,128)(2,1)}, u32[]{:S(2)}) copy-start(bf16[512,512]{1,0:T(8,128)(2,1)} %param.31) | copy-start | bytes 1572868
  7.2 7.9 %copy-start.5 = (bf16[256,512]{1,0:T(8,128)(2,1)S(1)}, bf16[256,512]{1,0:T(8,128)(2,1)}, u32[]{:S(2)}) copy-start(bf16[256,512]{1,0:T(8,128)(2,1)} %param.21) | copy-start | bytes 786436
  7.2 66.9 %reduce-scatter.2.cloned.1.call-start = ((), (), s32[]{:S(2)}) async-start(), calls=%async_computation.1 | async-start | bytes 163840 | tf_op jit(solution)/shard_map/reduce_scatter | solution.py:217
  11.0 7.6 %collective-permute-start = (bf16[128,512]{1,0:T(8,128)(2,1)S(1)}, bf16[128,512]{1,0:T(8,128)(2,1)S(1)}, u32[]{:S(2)}, u32[]{:S(2)}) collective-permute-start(bf16[128,512]{1,0:T(8,128)(2,1)S(1)} %get-tuple-element.22), channel_id=1, source_target_pairs={{0,4},{4,8},{8,12},{12,16},{16,20},{20,24},{24,28},{28,0},{1,5},{5... | collective-permute-start | bytes 393224 | tf_op jit(solution)/shard_map/ppermute | solution.py:38
  13.7 5.0 %collective-permute-start.1 = (bf16[128,512]{1,0:T(8,128)(2,1)S(1)}, bf16[128,512]{1,0:T(8,128)(2,1)S(1)}, u32[]{:S(2)}, u32[]{:S(2)}) collective-permute-start(bf16[128,512]{1,0:T(8,128)(2,1)S(1)} %get-tuple-element.23), channel_id=1, source_target_pairs={{4,0},{8,4},{12,8},{16,12},{20,16},{24,20},{28,24},{0,28},{5,1},{9... | collective-permute-start | bytes 393224 | tf_op jit(solution)/shard_map/ppermute | solution.py:39
  15.0 7.4 %copy-start.24 = (pred[768]{0:T(1024)(128)(4,1)}, pred[768]{0:T(1024)(128)(4,1)S(1)}, u32[]{:S(2)}) copy-start(pred[768]{0:T(1024)(128)(4,1)S(1)} %iota_compare_fusion.9) | copy-start | bytes 2308
  15.5 33.3 %copy-start.22 = (pred[768]{0:T(1024)(128)(4,1)}, pred[768]{0:T(1024)(128)(4,1)S(1)}, u32[]{:S(2)}) copy-start(pred[768]{0:T(1024)(128)(4,1)S(1)} %iota_compare_fusion.8) | copy-start | bytes 2308
  15.5 3.2 %copy-start.2 = (bf16[512,512]{1,0:T(8,128)(2,1)S(1)}, bf16[512,512]{1,0:T(8,128)(2,1)}, u32[]{:S(2)}) copy-start(bf16[512,512]{1,0:T(8,128)(2,1)} %param.20) | copy-start | bytes 1572868
  22.4 3.1 %copy-start.9 = (f32[512]{0:T(512)S(1)}, f32[512]{0:T(512)}, u32[]{:S(2)}) copy-start(f32[512]{0:T(512)} %param.33) | copy-start | bytes 6148
  25.3 3.8 %copy-start.4 = (bf16[512,512]{1,0:T(8,128)(2,1)S(1)}, bf16[512,512]{1,0:T(8,128)(2,1)}, u32[]{:S(2)}) copy-start(bf16[512,512]{1,0:T(8,128)(2,1)} %param.35) | copy-start | bytes 1572868
  25.3 8.2 %copy-start.1 = (bf16[512,512]{1,0:T(8,128)(2,1)S(1)}, bf16[512,512]{1,0:T(8,128)(2,1)}, u32[]{:S(2)}) copy-start(bf16[512,512]{1,0:T(8,128)(2,1)} %param.34) | copy-start | bytes 1572868
  25.5 8.3 %copy-start.11 = (f32[256]{0:T(256)}, f32[256]{0:T(256)S(1)}, u32[]{:S(2)}) copy-start(f32[256]{0:T(256)S(1)} %add_rsqrt_fusion.1) | copy-start | bytes 3076
  25.7 11.2 %collective-permute-start.4 = (bf16[16,512]{1,0:T(8,128)(2,1)S(1)}, bf16[16,512]{1,0:T(8,128)(2,1)S(1)}, u32[]{:S(2)}, u32[]{:S(2)}) collective-permute-start(bf16[16,512]{1,0:T(8,128)(2,1)S(1)} %get-tuple-element.21), channel_id=1, source_target_pairs={{1,0},{2,1},{3,2},{0,3},{5,4},{6,5},{7,6},{4,7},{9,8},{10,9},{11,1... | collective-permute-start | bytes 49160 | tf_op jit(solution)/shard_map/ppermute | solution.py:24
  29.1 4.4 %collective-permute-start.2 = (bf16[16,512]{1,0:T(8,128)(2,1)S(1)}, bf16[16,512]{1,0:T(8,128)(2,1)S(1)}, u32[]{:S(2)}, u32[]{:S(2)}) collective-permute-start(bf16[16,512]{1,0:T(8,128)(2,1)S(1)} %get-tuple-element.21), channel_id=1, source_target_pairs={{0,1},{1,2},{2,3},{3,0},{4,5},{5,6},{6,7},{7,4},{8,9},{9,10},{10,1... | collective-permute-start | bytes 49160 | tf_op jit(solution)/shard_map/ppermute | solution.py:22
  33.5 4.4 %collective-permute-start.3 = (bf16[16,512]{1,0:T(8,128)(2,1)S(1)}, bf16[16,512]{1,0:T(8,128)(2,1)S(1)}, u32[]{:S(2)}, u32[]{:S(2)}) collective-permute-start(bf16[16,512]{1,0:T(8,128)(2,1)S(1)} %collective-permute-done.2), channel_id=1, source_target_pairs={{0,1},{1,2},{2,3},{3,0},{4,5},{5,6},{6,7},{7,4},{8,9},{9,10},{10,1... | collective-permute-start | bytes 49160 | tf_op jit(solution)/shard_map/ppermute | solution.py:22
  41.8 3.2 %copy-start.3 = (bf16[256,512]{1,0:T(8,128)(2,1)S(1)}, bf16[256,512]{1,0:T(8,128)(2,1)}, u32[]{:S(2)}) copy-start(bf16[256,512]{1,0:T(8,128)(2,1)} %param.22) | copy-start | bytes 786436
  41.8 3.2 %copy-start.15 = (f32[512]{0:T(512)S(1)}, f32[512]{0:T(512)}, u32[]{:S(2)}) copy-start(f32[512]{0:T(512)} %param.37) | copy-start | bytes 6148
  48.8 4.1 %copy-start.17 = (s32[768]{0:T(1024)S(1)}, s32[768]{0:T(1024)}, u32[]{:S(2)}) copy-start(s32[768]{0:T(1024)} %param.27) | copy-start | bytes 9220
  55.0 20.0 %copy-start.12 = (f32[256]{0:T(256)S(1)}, f32[256]{0:T(256)}, u32[]{:S(2)}) copy-start(f32[256]{0:T(256)} %copy-done.11) | copy-start | bytes 3076
  75.4 2.7 %copy-start.23 = (bf16[512,512]{1,0:T(8,128)(2,1)S(1)}, bf16[512,512]{1,0:T(8,128)(2,1)}, u32[]{:S(2)}) copy-start(bf16[512,512]{1,0:T(8,128)(2,1)} %param.32) | copy-start | bytes 1572868
  75.4 2.7 %copy-start.25 = (pred[768]{0:T(1024)(128)(4,1)S(1)}, pred[768]{0:T(1024)(128)(4,1)}, u32[]{:S(2)}) copy-start(pred[768]{0:T(1024)(128)(4,1)} %copy-done.24) | copy-start | bytes 2308
  78.1 3.8 %copy-start.8 = (bf16[512,512]{1,0:T(8,128)(2,1)S(1)}, bf16[512,512]{1,0:T(8,128)(2,1)}, u32[]{:S(2)}) copy-start(bf16[512,512]{1,0:T(8,128)(2,1)} %param.31) | copy-start | bytes 1572868
  78.1 3.8 %copy-start.19 = (s32[768]{0:T(1024)S(1)}, s32[768]{0:T(1024)}, u32[]{:S(2)}) copy-start(s32[768]{0:T(1024)} %param.25) | copy-start | bytes 9220
  81.9 2.5 %copy-start.21 = (s32[768]{0:T(1024)S(1)}, s32[768]{0:T(1024)}, u32[]{:S(2)}) copy-start(s32[768]{0:T(1024)} %param.24) | copy-start | bytes 9220
  85.3 6.1 %collective-permute-start.5 = (bf16[128,512]{1,0:T(8,128)(2,1)S(1)}, bf16[128,512]{1,0:T(8,128)(2,1)S(1)}, u32[]{:S(2)}, u32[]{:S(2)}) collective-permute-start(bf16[128,512]{1,0:T(8,128)(2,1)S(1)} %get-tuple-element.18), channel_id=1, source_target_pairs={{0,4},{4,8},{8,12},{12,16},{16,20},{20,24},{24,28},{28,0},{1,5},{5... | collective-permute-start | bytes 393224 | tf_op jit(solution)/shard_map/ppermute | solution.py:38
  89.5 5.3 %copy-start.14 = (s32[256]{0:T(256)S(1)}, s32[256]{0:T(256)}, u32[]{:S(2)}) copy-start(s32[256]{0:T(256)} %copy-done.13) | copy-start | bytes 3076
  89.5 5.0 %collective-permute-start.6 = (bf16[128,512]{1,0:T(8,128)(2,1)S(1)}, bf16[128,512]{1,0:T(8,128)(2,1)S(1)}, u32[]{:S(2)}, u32[]{:S(2)}) collective-permute-start(bf16[128,512]{1,0:T(8,128)(2,1)S(1)} %get-tuple-element.19), channel_id=1, source_target_pairs={{4,0},{8,4},{12,8},{16,12},{20,16},{24,20},{28,24},{0,28},{5,1},{9... | collective-permute-start | bytes 393224 | tf_op jit(solution)/shard_map/ppermute | solution.py:39
  (3 other events, 4.0 us)
Sparse Core Ops, SparseCore 0:
  55.1 18.9 reduce-scatter.1
